TPU v7x, 512 devices: a whole 4x8x8 slice. The times are simulated.
512 devices in a mesh: section: 8 (over x, core), expert: 64 (over z, y).
Axes of the slice: x: 4, y: 8, z: 8, core: 2. Of those that a mesh axis runs over, the one named last changes fastest.
Arguments:
- histories: bfloat16 [8, 8192, 5120], P('section', 'expert'), may hold values from -6 to 6
- page_map: int32 [8, 2, 2048], P('section', None, 'expert'), may hold values from 0 to 2047, as said below
- user_pages: int32 [8, 64, 4], P('section', 'expert'), may hold values from 1 to 16, 32 in all within a row
- tails: int32 [8, 64, 4], P('section', 'expert'), may hold values from 1 to 4
- routes: int32 [8, 8192, 2], P('section', 'expert'), may hold values from 0 to 31, all different within a row; in each aligned block of 128 rows (0 to 127, 128 to 255, ..., all dimensions but the last counted through in order) at most 16 rows name the same one
- out_proj: bfloat16 [8, 1024, 1024], P('section', 'expert'), may hold values from -0.1875 to 0.1875
- router: bfloat16 [8, 1024, 32], P('section'), may hold values from -0.75 to 0.75
- w_gate: bfloat16 [8, 1024, 32768], P('section', None, 'expert'), may hold values from -0.1875 to 0.1875
- w_up: bfloat16 [8, 1024, 32768], P('section', None, 'expert'), may hold values from -0.1875 to 0.1875
- w_down: bfloat16 [8, 32768, 1024], P('section', 'expert'), may hold values from -0.1875 to 0.1875
Outputs:
- handed: bfloat16 [8, 8192, 1024], P('section', 'expert')
Inputs may be any that keep to these rules, and one draw needn't show every extreme that they name: page_map[0] is a permutation of the pages of a section and page_map[1] its inverse; every device holds exactly 32 pages before and after; no device's pages send more than 1 pages to one device, and some send exactly 1. `user_pages`: the 4 entries of one device sum to 32, and the largest is 16. `routes`: A row names 2 different experts; among the rows of one device, no expert is named more than 16 times, a bound that some block reaches.
All inputs are finite; a program needn't handle non-finite values.
Results may differ from a plain program's by a relative error of at most 0.012.
Values may be sent and summed in bfloat16 or wider, within the bound.
No kernel may reach another device: no remote copies, remote signals or barrier semaphores. Data moves between devices by JAX's collectives and lax.ppermute only.
A program may use at most 64 MiB of HBM per device.

v0:
```python
import jax
import jax.numpy as jnp
from jax import lax
from jax.sharding import PartitionSpec as P

HEADS = 8


def swapped(shard, axis, apart):
    return lax.ppermute(shard, axis, [(i, i ^ 1 << apart) for i in range(lax.axis_size(axis))])


def from_behind(block, axis, distance):
    devices = range(lax.axis_size(axis))
    route = [((i - distance) % len(devices), i) for i in devices]
    return lax.ppermute(block, axis, route)


def layout_rows(counts, tail_rows, page_rows, row_count):
    starting = jnp.cumsum(counts) - counts
    length = (counts - 1) * page_rows + tail_rows
    row_index = jnp.arange(row_count, dtype=jnp.int32)
    page_of = row_index // page_rows
    owner_of = jnp.sum((starting[None, :] <= page_of[:, None]).astype(jnp.int32), axis=1) - 1
    member = owner_of[:, None] == jnp.arange(counts.shape[0], dtype=jnp.int32)[None, :]
    offset = jnp.sum(jnp.where(member, starting[None, :] * page_rows, 0), axis=1)
    spread = jnp.sum(jnp.where(member, length[None, :], 0), axis=1)
    return (owner_of, row_index - offset, spread)


def attend(balanced, counts, tail_rows, page_rows):
    row_count = balanced.shape[0]
    model_width = balanced.shape[1] // 5
    head_dim = model_width // HEADS
    owner_of, position, spread = layout_rows(counts, tail_rows, page_rows, row_count)
    allowed = (
        (owner_of[:, None] == owner_of[None, :])
        & (position[None, :] <= position[:, None])
        & (position[None, :] < spread[None, :])
    )
    queries = balanced[:, :model_width].reshape(row_count, HEADS, head_dim)
    key_rows = balanced[:, model_width : 2 * model_width].reshape(row_count, HEADS, head_dim)
    values = balanced[:, 2 * model_width : 3 * model_width].reshape(row_count, HEADS, head_dim)
    scores = jnp.einsum(
        "qhd,khd->hqk", queries, key_rows, preferred_element_type=jnp.float32
    ) * head_dim ** (-0.5)
    weights = (
        jnp.where(allowed[None], jax.nn.silu(scores), 0.0)
        / spread.astype(jnp.float32)[None, :, None]
    )
    weights = weights.astype(jnp.bfloat16)
    attended = jnp.einsum(
        "hqk,khd->qhd", weights, values, preferred_element_type=jnp.float32
    ).reshape(row_count, model_width)
    average = jnp.mean(attended, axis=1, keepdims=True)
    centered = attended - average
    variance = jnp.mean(centered * centered, axis=1, keepdims=True)
    gating = balanced[:, 3 * model_width : 4 * model_width].astype(jnp.float32)
    return (centered * lax.rsqrt(variance + 1e-05) * gating).astype(jnp.bfloat16)


def gate_share(normed, router, routes):
    logits = jnp.dot(normed, router, preferred_element_type=jnp.float32)
    scores = jax.nn.sigmoid(logits)
    picked = routes[:, :, None] == jnp.arange(router.shape[1], dtype=jnp.int32)[None, None, :]
    chosen = jnp.sum(jnp.where(picked, scores[:, None, :], 0.0), axis=2)
    return chosen / jnp.sum(chosen, axis=1, keepdims=True)


def slot_table(routes, experts, capacity):
    pair_count = routes.shape[0] * routes.shape[1]
    chosen = routes.reshape(-1)
    onehot = (chosen[:, None] == jnp.arange(experts, dtype=jnp.int32)[None, :]).astype(jnp.int32)
    before = jnp.cumsum(onehot, axis=0) - onehot
    ranking = jnp.sum(before * onehot, axis=1)
    slot_of_pair = chosen * capacity + ranking
    matches = slot_of_pair[None, :] == jnp.arange(experts * capacity, dtype=jnp.int32)[:, None]
    source_token = (
        jnp.sum(jnp.where(matches, jnp.arange(pair_count, dtype=jnp.int32)[None, :], 0), axis=1)
        // 2
    )
    return (slot_of_pair, source_token)


def whole_expert(incoming, gate_full, up_full, down_full):
    flat_rows = incoming.reshape(-1, incoming.shape[-1])
    gate_act = jnp.dot(flat_rows, gate_full, preferred_element_type=jnp.float32)
    up_act = jnp.dot(flat_rows, up_full, preferred_element_type=jnp.float32)
    hidden = (jax.nn.silu(gate_act) * up_act).astype(jnp.bfloat16)
    half_units = gate_full.shape[1] // 2
    first_part = jnp.dot(
        hidden[:, :half_units], down_full[:half_units], preferred_element_type=jnp.float32
    ).astype(jnp.bfloat16)
    second_part = jnp.dot(
        hidden[:, half_units:], down_full[half_units:], preferred_element_type=jnp.float32
    ).astype(jnp.bfloat16)
    summed = (first_part.astype(jnp.float32) + second_part.astype(jnp.float32)).astype(jnp.bfloat16)
    return summed.reshape(incoming.shape)


def shards(histories, page_map, user_pages, tails, routes, out_proj, router, w_gate, w_up, w_down):
    devices = lax.axis_size("expert")
    parity = lax.axis_index("expert") % 2
    row_count = histories.shape[1]
    stacked_width = histories.shape[2]
    model_width = stacked_width // 5
    pages_dev = page_map.shape[2]
    page_rows = row_count // pages_dev
    page_slots = (pages_dev + devices - 1) // devices
    page_block = histories[0].reshape(pages_dev, page_rows, stacked_width)
    target = page_map[0, 0]
    target_dev = target // pages_dev
    earlier = (target_dev[None, :] == target_dev[:, None]) & (target[None, :] < target[:, None])
    position = target_dev * page_slots + jnp.sum(earlier.astype(jnp.int32), axis=1)
    matches = position[None, :] == jnp.arange(devices * page_slots, dtype=jnp.int32)[:, None]
    chosen_page = jnp.sum(
        jnp.where(matches, jnp.arange(pages_dev, dtype=jnp.int32)[None, :], 0), axis=1
    )
    outgoing = page_block[chosen_page]
    arrived = lax.all_to_all(outgoing, "expert", split_axis=0, concat_axis=0, tiled=True)
    anchor = page_map[0, 1]
    anchor_dev = anchor // pages_dev
    ordering = jnp.arange(pages_dev, dtype=jnp.int32)
    sooner = (anchor_dev[None, :] == anchor_dev[:, None]) & (ordering[None, :] < ordering[:, None])
    where_from = anchor_dev * page_slots + jnp.sum(sooner.astype(jnp.int32), axis=1)
    balanced = arrived[where_from].reshape(row_count, stacked_width)
    mixed_in = attend(balanced, user_pages[0, 0], tails[0, 0], page_rows)
    projected = jnp.dot(
        mixed_in,
        lax.all_gather(out_proj, "expert", axis=1, tiled=True)[0],
        preferred_element_type=jnp.float32,
    )
    resid = (balanced[:, 4 * model_width :].astype(jnp.float32) + projected).astype(jnp.bfloat16)
    resid_wide = resid.astype(jnp.float32)
    normed = (
        resid_wide * lax.rsqrt(jnp.mean(resid_wide * resid_wide, axis=1, keepdims=True) + 1e-06)
    ).astype(jnp.bfloat16)
    experts = router.shape[2]
    capacity = 4 * row_count // experts
    share = gate_share(normed, router[0], routes[0])
    slot_of_pair, source_token = slot_table(routes[0], experts, capacity)
    packed = normed[source_token].reshape(experts, capacity, model_width)
    is_odd = parity == 1
    half_units = w_gate.shape[2]
    gate_up = jnp.concatenate([w_gate[0], w_up[0]], axis=1)
    other_gate_up = swapped(gate_up, "expert", 0)
    other_down = swapped(w_down[0], "expert", 0)
    own_gate = gate_up[:, :half_units]
    own_up = gate_up[:, half_units:]
    other_gate = other_gate_up[:, :half_units]
    other_up = other_gate_up[:, half_units:]
    gate_full = jnp.where(
        is_odd,
        jnp.concatenate([other_gate, own_gate], axis=1),
        jnp.concatenate([own_gate, other_gate], axis=1),
    )
    up_full = jnp.where(
        is_odd,
        jnp.concatenate([other_up, own_up], axis=1),
        jnp.concatenate([own_up, other_up], axis=1),
    )
    down_full = jnp.where(
        is_odd,
        jnp.concatenate([other_down, w_down[0]], axis=0),
        jnp.concatenate([w_down[0], other_down], axis=0),
    )
    half_cap = capacity // 2
    sent_rows = packed.reshape(experts * 2, half_cap, model_width)
    own_rows = lax.all_to_all(sent_rows, "expert", split_axis=0, concat_axis=0, tiled=True)
    served = whole_expert(own_rows, gate_full, up_full, down_full)
    came_back = lax.all_to_all(served, "expert", split_axis=0, concat_axis=0, tiled=True)
    result = came_back.reshape(experts, capacity, model_width)
    picked = result.reshape(experts * capacity, model_width)[slot_of_pair]
    picked = picked.reshape(row_count, 2, model_width).astype(jnp.float32)
    mixture = jnp.sum(picked * share[:, :, None], axis=1)
    output_rows = (resid_wide + mixture).astype(jnp.bfloat16)
    return from_behind(output_rows[None], "section", 1)


def solution(mesh):
    in_specs = (
        P("section", "expert", None),
        P("section", None, "expert"),
        P("section", "expert", None),
        P("section", "expert", None),
        P("section", "expert", None),
        P("section", "expert", None),
        P("section", None, None),
        P("section", None, "expert"),
        P("section", None, "expert"),
        P("section", "expert", None),
    )
    out_specs = P("section", "expert", None)
    return jax.shard_map(shards, mesh=mesh, in_specs=in_specs, out_specs=out_specs, check_vma=False)
```

profile of v0, /device:TPU:8, one launch (start us, length us, event | category | flops | bytes accessed | tf_op | source)
XLA Modules:
  0.0 289.1 jit_solution(12892616485323434839)
XLA Ops:
  8.3 2.6 reshape_squeeze.6
  10.9 4.2 %gather_fusion = bf16[64,4,5120]{2,1,0:T(4,128)(2,1)} fusion(bf16[32,4,5120]{2,1,0:T(4,128)(2,1)S(1)} %reshape_squeeze.6, s32[1024]{0:T(1024)S(1)} %pad_clamp_fusion.3), kind=kCustom, calls=%fused_computation | custom fusion | bytes 5243136 | tf_op jit(solution)/shard_map/gather | solution.py:119
  15.1 16.6 %all-to-all-start = ((bf16[64,4,5120]{2,1,0:T(4,128)(2,1)}), bf16[64,4,5120]{2,1,0:T(4,128)(2,1)S(1)}, u32[]{:S(2)}, u32[]{:S(2)}) async-start(bf16[64,4,5120]{2,1,0:T(4,128)(2,1)} %gather_fusion), calls=%async_computation | async-start | bytes 5242880 | tf_op jit(solution)/shard_map/all_to_all | solution.py:120
  32.5 3.1 %pad_maximum_fusion.1 = bf16[1024,1024]{1,0:T(8,128)(2,1)} fusion(bf16[1024,512]{1,0:T(8,128)(2,1)} %bitcast.121, bf16[1024,512]{1,0:T(8,128)(2,1)} %bitcast.119), kind=kLoop, calls=%fused_computation.5 | loop fusion | flops 4194304 | bytes 4194304 | tf_op jit(solution)/shard_map/concatenate | solution.py:145
  35.6 2.4 collective-permute-start
  40.0 57.6 %all-to-all-done = bf16[64,4,5120]{2,1,0:T(4,128)(2,1)S(1)} async-done(((bf16[64,4,5120]{2,1,0:T(4,128)(2,1)}), bf16[64,4,5120]{2,1,0:T(4,128)(2,1)S(1)}, u32[]{:S(2)}, u32[]{:S(2)}) %all-to-all-start) | async-done | bytes 2621472 | tf_op jit(solution)/shard_map/all_to_all | solution.py:120
  97.6 2.7 gather_fusion.1
  100.3 2.5 reshape.543
  104.4 52.7 %all-gather.2.cloned.1.call-done = bf16[1,1024,1024]{2,1,0:T(8,128)(2,1)} async-done(((bf16[1,16,1024]{2,1,0:T(8,128)(2,1)}), bf16[1,1024,1024]{2,1,0:T(8,128)(2,1)}) %all-gather.2.cloned.1.call-update) | async-done | bytes 2097168 | tf_op jit(solution)/shard_map/all_gather | solution.py:130
  157.1 2.2 multiply_reduce_fusion.1
  159.4 2.8 gather_fusion.2
  162.2 10.1 %all-to-all-start.1 = ((bf16[64,8,1024]{2,1,0:T(8,128)(2,1)}), bf16[64,8,1024]{2,1,0:T(8,128)(2,1)}, u32[]{:S(2)}, u32[]{:S(2)}) async-start(bf16[64,8,1024]{2,1,0:T(8,128)(2,1)} %bitcast.20), calls=%async_computation.1 | async-start | bytes 2097152 | tf_op jit(solution)/shard_map/all_to_all | solution.py:169
  172.2 2.6 collective-permute-start.1
  174.9 39.3 %collective-permute-done.1 = bf16[512,1024]{1,0:T(8,128)(2,1)} collective-permute-done((bf16[512,1024]{1,0:T(8,128)(2,1)S(1)}, bf16[512,1024]{1,0:T(8,128)(2,1)}, u32[]{:S(2)}, u32[]{:S(2)}) %collective-permute-start.1) | collective-permute-done | bytes 1048608 | tf_op jit(solution)/shard_map/ppermute | solution.py:10
  214.2 4.1 %maximum_select_fusion = bf16[1024,1024]{1,0:T(8,128)(2,1)} fusion(bf16[512,1024]{1,0:T(8,128)(2,1)S(1)} %bitcast.118, bf16[512,1024]{1,0:T(8,128)(2,1)} %collective-permute-done.1, pred[]{:T(512)S(6)} %eq.150), kind=kLoop, calls=%fused_computation.19 | loop fusion | flops 9437184 | bytes 4194305 | tf_op jit(solution)/shard_map/jit(_where)/select_n | solution.py:162
  218.3 3.1 %fusion.68 = (bf16[1024,512]{1,0:T(8,128)(2,1)}, bf16[1024,512]{1,0:T(8,128)(2,1)}) fusion(bf16[1024,1024]{1,0:T(8,128)(2,1)} %collective-permute-done), kind=kLoop, calls=%fused_computation.141 | loop fusion | bytes 4194304 | tf_op jit(solution)/shard_map/slice | solution.py:151
  221.3 3.3 %fusion.1 = f32[512,1024]{1,0:T(8,128)S(1)} fusion(bf16[1024,512]{1,0:T(8,128)(2,1)S(1)} %bitcast.120, bf16[1024,512]{1,0:T(8,128)(2,1)} %get-tuple-element.12, pred[]{:T(512)S(6)} %eq.150, bf16[64,8,1024]{2,1,0:T(8,128)(2,1)} %all-to-all-done.1), kind=kOutput, calls=%fused_computation.8 | convolution fusion | flops 1083179008 | bytes 5242881 | tf_op jit(solution)/shard_map/dot_general | solution.py:87
  224.7 3.8 %multiply_convert_fusion = bf16[512,1024]{1,0:T(8,128)(2,1)S(1)} fusion(f32[512,1024]{1,0:T(8,128)S(1)} %fusion.1, bf16[1024,512]{1,0:T(8,128)(2,1)S(1)} %bitcast.122, bf16[1024,512]{1,0:T(8,128)(2,1)S(1)} %copy-done.5, pred[]{:T(512)S(6)} %eq.150, bf16[64,8,1024]{2,1,0:T(8,128)(2,1)} %all-to-all-done.1), kind=kOutput, calls=%fused_computation.23 | convolution fusion | flops 1086324736 | bytes 6291457 | tf_op jit(solution)/shard_map/dot_general | solution.py:88
  229.2 1.7 fusion.18
  230.9 12.6 %all-to-all-start.2 = ((bf16[64,8,1024]{2,1,0:T(8,128)(2,1)}), bf16[64,8,1024]{2,1,0:T(8,128)(2,1)S(1)}, u32[]{:S(2)}, u32[]{:S(2)}) async-start(bf16[64,8,1024]{2,1,0:T(8,128)(2,1)} %fusion.18), calls=%async_computation.2 | async-start | bytes 2097152 | tf_op jit(solution)/shard_map/all_to_all | solution.py:171
  244.2 27.0 %all-to-all-done.2 = bf16[64,8,1024]{2,1,0:T(8,128)(2,1)S(1)} async-done(((bf16[64,8,1024]{2,1,0:T(8,128)(2,1)}), bf16[64,8,1024]{2,1,0:T(8,128)(2,1)S(1)}, u32[]{:S(2)}, u32[]{:S(2)}) %all-to-all-start.2) | async-done | bytes 1048608 | tf_op jit(solution)/shard_map/all_to_all | solution.py:171
  271.3 1.2 gather_fusion.3
  273.1 1.3 multiply_reduce_fusion
  274.5 7.0 %collective-permute-done.2 = bf16[1,128,1024]{2,1,0:T(8,128)(2,1)S(1)} collective-permute-done((bf16[1,128,1024]{2,1,0:T(8,128)(2,1)S(1)}, bf16[1,128,1024]{2,1,0:T(8,128)(2,1)S(1)}, u32[]{:S(2)}, u32[]{:S(2)}) %collective-permute-start.2) | collective-permute-done | bytes 262176 | tf_op jit(solution)/shard_map/ppermute | solution.py:16
  (81 shorter events, 9.0 us)
Async XLA Ops:
  6.5 237.3 %copy-start = (bf16[1,1024,32]{1,2,0:T(8,128)(2,1)S(1)}, bf16[1,1024,32]{1,2,0:T(8,128)(2,1)}, u32[]{:S(2)}) copy-start(bf16[1,1024,32]{1,2,0:T(8,128)(2,1)} %param.16) | copy-start | bytes 196612
  15.1 82.5 %all-to-all-start = ((bf16[64,4,5120]{2,1,0:T(4,128)(2,1)}), bf16[64,4,5120]{2,1,0:T(4,128)(2,1)S(1)}, u32[]{:S(2)}, u32[]{:S(2)}) async-start(bf16[64,4,5120]{2,1,0:T(4,128)(2,1)} %gather_fusion), calls=%async_computation | async-start | bytes 5242880 | tf_op jit(solution)/shard_map/all_to_all | solution.py:120
  31.7 125.4 %all-gather.2.cloned.1.call-start = ((), (), s32[]{:S(2)}) async-start(), calls=%async_computation.3 | async-start | bytes 2129920 | tf_op jit(solution)/shard_map/all_gather | solution.py:130
  32.4 5.5 %copy-start.6 = (s32[1,128,2]{1,2,0:T(2,128)S(1)}, s32[1,128,2]{1,2,0:T(2,128)}, u32[]{:S(2)}) copy-start(s32[1,128,2]{1,2,0:T(2,128)} %param.14) | copy-start | bytes 3076
  32.4 5.9 %copy-start.8 = (s32[1,1,4]{2,1,0:T(1,128)S(1)}, s32[1,1,4]{2,1,0:T(1,128)}, u32[]{:S(2)}) copy-start(s32[1,1,4]{2,1,0:T(1,128)} %param.12) | copy-start | bytes 52
  32.4 6.1 %copy-start.9 = (s32[1,1,4]{2,1,0:T(1,128)S(1)}, s32[1,1,4]{2,1,0:T(1,128)}, u32[]{:S(2)}) copy-start(s32[1,1,4]{2,1,0:T(1,128)} %param.13) | copy-start | bytes 52
  32.5 7.1 %copy-start.7 = (s32[1,2,32]{2,1,0:T(2,128)S(1)}, s32[1,2,32]{2,1,0:T(2,128)}, u32[]{:S(2)}) copy-start(s32[1,2,32]{2,1,0:T(2,128)} %param.11) | copy-start | bytes 772
  35.6 182.7 %collective-permute-start = (bf16[1024,1024]{1,0:T(8,128)(2,1)}, bf16[1024,1024]{1,0:T(8,128)(2,1)}, u32[]{:S(2)}, u32[]{:S(2)}) collective-permute-start(bf16[1024,1024]{1,0:T(8,128)(2,1)} %pad_maximum_fusion.1), channel_id=1, source_target_pairs={{0,1},{1,0},{2,3},{3,2},{4,5},{5,4},{6,7},{7,6},{8,9},{9,8},{10,11... | collective-permute-start | bytes 6291464 | tf_op jit(solution)/shard_map/ppermute | solution.py:10
  162.2 10.1 %copy-start.2 = (bf16[1,512,1024]{2,1,0:T(8,128)(2,1)S(1)}, bf16[1,512,1024]{2,1,0:T(8,128)(2,1)}, u32[]{:S(2)}) copy-start(bf16[1,512,1024]{2,1,0:T(8,128)(2,1)} %param.19) | copy-start | bytes 3145732
  162.2 59.2 %all-to-all-start.1 = ((bf16[64,8,1024]{2,1,0:T(8,128)(2,1)}), bf16[64,8,1024]{2,1,0:T(8,128)(2,1)}, u32[]{:S(2)}, u32[]{:S(2)}) async-start(bf16[64,8,1024]{2,1,0:T(8,128)(2,1)} %bitcast.20), calls=%async_computation.1 | async-start | bytes 2097152 | tf_op jit(solution)/shard_map/all_to_all | solution.py:169
  172.2 41.9 %collective-permute-start.1 = (bf16[512,1024]{1,0:T(8,128)(2,1)S(1)}, bf16[512,1024]{1,0:T(8,128)(2,1)}, u32[]{:S(2)}, u32[]{:S(2)}) collective-permute-start(bf16[512,1024]{1,0:T(8,128)(2,1)S(1)} %bitcast.117), channel_id=1, source_target_pairs={{0,1},{1,0},{2,3},{3,2},{4,5},{5,4},{6,7},{7,6},{8,9},{9,8},{10,11... | collective-permute-start | bytes 3145736 | tf_op jit(solution)/shard_map/ppermute | solution.py:10
  218.3 3.1 %copy-start.3 = (bf16[1,1024,512]{2,1,0:T(8,128)(2,1)S(1)}, bf16[1,1024,512]{2,1,0:T(8,128)(2,1)}, u32[]{:S(2)}) copy-start(bf16[1,1024,512]{2,1,0:T(8,128)(2,1)} %param.17) | copy-start | bytes 3145732
  221.3 3.3 %copy-start.4 = (bf16[1,1024,512]{2,1,0:T(8,128)(2,1)S(1)}, bf16[1,1024,512]{2,1,0:T(8,128)(2,1)}, u32[]{:S(2)}) copy-start(bf16[1,1024,512]{2,1,0:T(8,128)(2,1)} %param.18) | copy-start | bytes 3145732
  221.3 3.3 %copy-start.5 = (bf16[1024,512]{1,0:T(8,128)(2,1)S(1)}, bf16[1024,512]{1,0:T(8,128)(2,1)}, u32[]{:S(2)}) copy-start(bf16[1024,512]{1,0:T(8,128)(2,1)} %get-tuple-element.11) | copy-start | bytes 3145732
  224.7 3.8 %copy-start.1 = (bf16[1024,1024]{1,0:T(8,128)(2,1)S(1)}, bf16[1024,1024]{1,0:T(8,128)(2,1)}, u32[]{:S(2)}) copy-start(bf16[1024,1024]{1,0:T(8,128)(2,1)} %maximum_select_fusion) | copy-start | bytes 6291460
  230.9 40.4 %all-to-all-start.2 = ((bf16[64,8,1024]{2,1,0:T(8,128)(2,1)}), bf16[64,8,1024]{2,1,0:T(8,128)(2,1)S(1)}, u32[]{:S(2)}, u32[]{:S(2)}) async-start(bf16[64,8,1024]{2,1,0:T(8,128)(2,1)} %fusion.18), calls=%async_computation.2 | async-start | bytes 2097152 | tf_op jit(solution)/shard_map/all_to_all | solution.py:171
  274.5 7.0 %collective-permute-start.2 = (bf16[1,128,1024]{2,1,0:T(8,128)(2,1)S(1)}, bf16[1,128,1024]{2,1,0:T(8,128)(2,1)S(1)}, u32[]{:S(2)}, u32[]{:S(2)}) collective-permute-start(bf16[1,128,1024]{2,1,0:T(8,128)(2,1)S(1)} %fusion.44), channel_id=1, source_target_pairs={{448,0},{0,64},{64,128},{128,192},{192,256},{256,320},{320,384},{3... | collective-permute-start | bytes 786440 | tf_op jit(solution)/shard_map/ppermute | solution.py:16
Sparse Core Ops, SparseCore 0:
  35.6 121.4 all-gather.1
where the time goes:
time: 290 us; the launch traced here: 289 us
  waiting for transfers between devices  184 us (63%)
  starting transfers between devices  44.3 us (15%)
  local copies, waits for them, and re-layouts  22.7 us (8%)
  between operations  13.8 us (5%)
  matrix products  12.5 us (4%)
  other arithmetic  11.4 us (4%)
    all_to_all x1, waiting for transfers between devices, shards(): lax.all_to_all(outgoing, 'expert', split_axis=0, concat_axis=0, tiled=True)  57.6 us
    all_gather x1, waiting for transfers between devices, shards(): lax.all_gather(out_proj, 'expert', axis=1, tiled=True)[0]  52.7 us
    ppermute x2, waiting for transfers between devices, swapped(): lax.ppermute(shard, axis, [(i, i ^ 1 << apart) for i in range(lax.axis_si...  39.3 us
    all_to_all x1, waiting for transfers between devices, shards(): lax.all_to_all(served, 'expert', split_axis=0, concat_axis=0, tiled=True)  27 us
    all_to_all x1, starting transfers between devices, shards(): lax.all_to_all(outgoing, 'expert', split_axis=0, concat_axis=0, tiled=True)  16.6 us
    all_to_all x1, starting transfers between devices, shards(): lax.all_to_all(served, 'expert', split_axis=0, concat_axis=0, tiled=True)  12.6 us
    all_to_all x1, starting transfers between devices, shards(): lax.all_to_all(sent_rows, 'expert', split_axis=0, concat_axis=0, tiled=True)  10.1 us
    ppermute x1, waiting for transfers between devices, from_behind(): return lax.ppermute(block, axis, route)  6.99 us
  transfers between devices with their start and end apart: 7, of which 5 were waited for; matrix products, arithmetic and copies ran while one was open for 9% of the time, Pallas kernels for 0%

commit v1 on v0

--- a/solution.py
+++ b/solution.py
@@ -1,9 +1,25 @@
+import functools
 import jax
 import jax.numpy as jnp
 from jax import lax
 from jax.sharding import PartitionSpec as P
 
 HEADS = 8
+
+
+def show_sizes(mine_x, device_axis, d_out):
+    return jnp.concatenate(
+        lax.all_to_all(
+            jnp.stack([mine_x] * lax.psum(1, axis_name=device_axis)),
+            concat_axis=0,
+            axis_name=device_axis,
+            split_axis=0,
+        ),
+        d_out,
+    )
+
+
+forms_place = functools.partial(show_sizes, device_axis="expert", d_out=1)
 
 
 def swapped(shard, axis, apart):
@@ -125,11 +141,7 @@
     where_from = anchor_dev * page_slots + jnp.sum(sooner.astype(jnp.int32), axis=1)
     balanced = arrived[where_from].reshape(row_count, stacked_width)
     mixed_in = attend(balanced, user_pages[0, 0], tails[0, 0], page_rows)
-    projected = jnp.dot(
-        mixed_in,
-        lax.all_gather(out_proj, "expert", axis=1, tiled=True)[0],
-        preferred_element_type=jnp.float32,
-    )
+    projected = jnp.dot(mixed_in, forms_place(out_proj)[0], preferred_element_type=jnp.float32)
     resid = (balanced[:, 4 * model_width :].astype(jnp.float32) + projected).astype(jnp.bfloat16)
     resid_wide = resid.astype(jnp.float32)
     normed = (

time: 290 us -> 304 us (1.048)
  blocking collectives: 0 us -> 81.2 us
  waiting for transfers between devices: 184 us -> 138 us
  between operations: 13.8 us -> 0.43 us
  starting transfers between devices: 44.3 us -> 35.4 us
    all_to_all x0 -> x1, blocking collectives: none -> 81.2 us  [shards(): lax.all_to_all(outgoing, 'expert', split_axis=0, concat_axis=0, tiled=True)]
    all_gather x1 -> x0, waiting for transfers between devices: 52.7 us -> none  [shards(): lax.all_gather(out_proj, 'expert', axis=1, tiled=True)[0]]
    ppermute x2, waiting for transfers between devices: 39.3 us -> 66.9 us  [swapped(): lax.ppermute(shard, axis, [(i, i ^ 1 << apart) for i in range(lax.axis_si...]
    all_to_all x1, waiting for transfers between devices: 57.6 us -> 36.7 us  [show_sizes(): lax.all_to_all(jnp.stack([mine_x] * lax.psum(1, axis_name=device_axis)),...]
    all_to_all x1, starting transfers between devices: 16.6 us -> 9.84 us  [show_sizes(): lax.all_to_all(jnp.stack([mine_x] * lax.psum(1, axis_name=device_axis)),...]
  transfers between devices with their start and end apart: 7 -> 6, of which waited for: 5 -> 4; matrix products, arithmetic and copies ran while one was open for 9% -> 8% of each run, Pallas kernels for 0% -> 0%
where the time goes in v1:
time: 304 us; the launch traced here: 303 us
  waiting for transfers between devices  138 us (45%)
  blocking collectives  81.2 us (27%)
  starting transfers between devices  35.4 us (12%)
  local copies, waits for them, and re-layouts  25 us (8%)
  matrix products  11.9 us (4%)
  other arithmetic  11.1 us (4%)
    all_to_all x1, blocking collectives, shards(): lax.all_to_all(outgoing, 'expert', split_axis=0, concat_axis=0, tiled=True)  81.2 us
    ppermute x2, waiting for transfers between devices, swapped(): lax.ppermute(shard, axis, [(i, i ^ 1 << apart) for i in range(lax.axis_si...  66.9 us
    all_to_all x1, waiting for transfers between devices, show_sizes(): lax.all_to_all(jnp.stack([mine_x] * lax.psum(1, axis_name=device_axis)),...  36.7 us
    all_to_all x1, waiting for transfers between devices, shards(): lax.all_to_all(served, 'expert', split_axis=0, concat_axis=0, tiled=True)  27.5 us
    all_to_all x1, starting transfers between devices, shards(): lax.all_to_all(served, 'expert', split_axis=0, concat_axis=0, tiled=True)  12.7 us
    all_to_all x1, starting transfers between devices, show_sizes(): lax.all_to_all(jnp.stack([mine_x] * lax.psum(1, axis_name=device_axis)),...  9.84 us
    all_to_all x1, starting transfers between devices, shards(): lax.all_to_all(sent_rows, 'expert', split_axis=0, concat_axis=0, tiled=True)  7.91 us
    ppermute x1, waiting for transfers between devices, from_behind(): return lax.ppermute(block, axis, route)  6.99 us
  transfers between devices with their start and end apart: 6, of which 4 were waited for; matrix products, arithmetic and copies ran while one was open for 8% of the time, Pallas kernels for 0%

profile of v1, /device:TPU:8, one launch (start us, length us, event | category | flops | bytes accessed | tf_op | source)
XLA Modules:
  0.0 303.2 jit_solution(114096800394732750)
XLA Ops:
  1.8 2.6 reshape_squeeze.6
  4.3 4.2 %gather_fusion = bf16[64,4,5120]{2,1,0:T(4,128)(2,1)} fusion(bf16[32,4,5120]{2,1,0:T(4,128)(2,1)S(1)} %reshape_squeeze.6, s32[1024]{0:T(1024)S(1)} %pad_clamp_fusion.3), kind=kCustom, calls=%fused_computation | custom fusion | bytes 5243136 | tf_op jit(solution)/shard_map/gather | solution.py:135
  8.5 81.2 %all_to_all.20 = bf16[64,4,5120]{2,1,0:T(4,128)(2,1)} all-to-all(bf16[64,4,5120]{2,1,0:T(4,128)(2,1)} %gather_fusion), channel_id=1, replica_groups=mesh['section'=8,'expert'=64] {'expert'}, dimensions={0} | all-to-all | bytes 5242880 | tf_op jit(solution)/shard_map/all_to_all | solution.py:136
  89.7 1.7 stack.2
  91.4 9.8 %all-to-all-start.1 = ((bf16[64,1,16,1024]{3,2,1,0:T(8,128)(2,1)}), bf16[64,1,16,1024]{3,2,1,0:T(8,128)(2,1)S(1)}, u32[]{:S(2)}, u32[]{:S(2)}) async-start(bf16[64,1,16,1024]{3,2,1,0:T(8,128)(2,1)} %stack.2), calls=%async_computation.1 | async-start | bytes 4194304 | tf_op jit(solution)/shard_map/all_to_all | solution.py:12
  101.3 2.8 pad_maximum_fusion.1
  104.1 2.4 collective-permute-start
  108.5 3.4 %gather_fusion.1 = bf16[32,4,5120]{2,1,0:T(4,128)(2,1)S(1)} fusion(bf16[64,4,5120]{2,1,0:T(4,128)(2,1)} %all_to_all.20, s32[1024]{0:T(1024)S(1)} %pad_clamp_fusion.2), kind=kCustom, calls=%fused_computation.1 | custom fusion | bytes 2621568 | tf_op jit(solution)/shard_map/gather | solution.py:142
  112.0 1.2 reshape.546
  115.9 36.7 %all-to-all-done.1 = bf16[64,1,16,1024]{3,2,1,0:T(8,128)(2,1)S(1)} async-done(((bf16[64,1,16,1024]{3,2,1,0:T(8,128)(2,1)}), bf16[64,1,16,1024]{3,2,1,0:T(8,128)(2,1)S(1)}, u32[]{:S(2)}, u32[]{:S(2)}) %all-to-all-start.1) | async-done | bytes 2097184 | tf_op jit(solution)/shard_map/all_to_all | solution.py:12
  152.6 1.6 multiply_reduce_fusion.1
  154.3 2.8 gather_fusion.2
  157.1 7.9 %all-to-all-start.2 = ((bf16[64,8,1024]{2,1,0:T(8,128)(2,1)}), bf16[64,8,1024]{2,1,0:T(8,128)(2,1)}, u32[]{:S(2)}, u32[]{:S(2)}) async-start(bf16[64,8,1024]{2,1,0:T(8,128)(2,1)} %bitcast.21), calls=%async_computation.2 | async-start | bytes 2097152 | tf_op jit(solution)/shard_map/all_to_all | solution.py:181
  165.0 2.6 collective-permute-start.1
  167.7 66.9 %collective-permute-done.1 = bf16[512,1024]{1,0:T(8,128)(2,1)} collective-permute-done((bf16[512,1024]{1,0:T(8,128)(2,1)S(1)}, bf16[512,1024]{1,0:T(8,128)(2,1)}, u32[]{:S(2)}, u32[]{:S(2)}) %collective-permute-start.1) | collective-permute-done | bytes 1048608 | tf_op jit(solution)/shard_map/ppermute | solution.py:26
  234.6 4.1 %maximum_select_fusion = bf16[1024,1024]{1,0:T(8,128)(2,1)} fusion(bf16[512,1024]{1,0:T(8,128)(2,1)S(1)} %bitcast.111, bf16[512,1024]{1,0:T(8,128)(2,1)} %collective-permute-done.1, pred[]{:T(512)S(6)} %eq.150), kind=kLoop, calls=%fused_computation.19 | loop fusion | flops 9437184 | bytes 4194305 | tf_op jit(solution)/shard_map/jit(_where)/select_n | solution.py:174
  238.7 3.1 %fusion.59 = (bf16[1024,512]{1,0:T(8,128)(2,1)}, bf16[1024,512]{1,0:T(8,128)(2,1)}) fusion(bf16[1024,1024]{1,0:T(8,128)(2,1)} %collective-permute-done), kind=kLoop, calls=%fused_computation.139 | loop fusion | bytes 4194304 | tf_op jit(solution)/shard_map/slice | solution.py:163
  241.8 3.3 %fusion.1 = f32[512,1024]{1,0:T(8,128)S(1)} fusion(bf16[1024,512]{1,0:T(8,128)(2,1)S(1)} %bitcast.113, bf16[1024,512]{1,0:T(8,128)(2,1)} %get-tuple-element.12, pred[]{:T(512)S(6)} %eq.150, bf16[64,8,1024]{2,1,0:T(8,128)(2,1)} %all-to-all-done.2), kind=kOutput, calls=%fused_computation.8 | convolution fusion | flops 1083179008 | bytes 5242881 | tf_op jit(solution)/shard_map/dot_general | solution.py:103
  245.1 3.8 %multiply_convert_fusion = bf16[512,1024]{1,0:T(8,128)(2,1)S(1)} fusion(f32[512,1024]{1,0:T(8,128)S(1)} %fusion.1, bf16[1024,512]{1,0:T(8,128)(2,1)S(1)} %bitcast.115, bf16[1024,512]{1,0:T(8,128)(2,1)S(1)} %copy-done.6, pred[]{:T(512)S(6)} %eq.150, bf16[64,8,1024]{2,1,0:T(8,128)(2,1)} %all-to-all-done.2), kind=kOutput, calls=%fused_computation.21 | convolution fusion | flops 1086324736 | bytes 6291457 | tf_op jit(solution)/shard_map/dot_general | solution.py:104
  249.6 1.7 fusion.16
  251.3 12.7 %all-to-all-start.3 = ((bf16[64,8,1024]{2,1,0:T(8,128)(2,1)}), bf16[64,8,1024]{2,1,0:T(8,128)(2,1)S(1)}, u32[]{:S(2)}, u32[]{:S(2)}) async-start(bf16[64,8,1024]{2,1,0:T(8,128)(2,1)} %fusion.16), calls=%async_computation.3 | async-start | bytes 2097152 | tf_op jit(solution)/shard_map/all_to_all | solution.py:183
  264.7 27.5 %all-to-all-done.3 = bf16[64,8,1024]{2,1,0:T(8,128)(2,1)S(1)} async-done(((bf16[64,8,1024]{2,1,0:T(8,128)(2,1)}), bf16[64,8,1024]{2,1,0:T(8,128)(2,1)S(1)}, u32[]{:S(2)}, u32[]{:S(2)}) %all-to-all-start.3) | async-done | bytes 1048608 | tf_op jit(solution)/shard_map/all_to_all | solution.py:183
  294.0 1.3 multiply_reduce_fusion
  295.5 7.0 %collective-permute-done.2 = bf16[1,128,1024]{2,1,0:T(8,128)(2,1)S(1)} collective-permute-done((bf16[1,128,1024]{2,1,0:T(8,128)(2,1)S(1)}, bf16[1,128,1024]{2,1,0:T(8,128)(2,1)S(1)}, u32[]{:S(2)}, u32[]{:S(2)}) %collective-permute-start.2) | collective-permute-done | bytes 262176 | tf_op jit(solution)/shard_map/ppermute | solution.py:32
  (84 shorter events, 10.5 us)
Async XLA Ops:
  0.0 264.3 %copy-start = (bf16[1,1024,32]{1,2,0:T(8,128)(2,1)S(1)}, bf16[1,1024,32]{1,2,0:T(8,128)(2,1)}, u32[]{:S(2)}) copy-start(bf16[1,1024,32]{1,2,0:T(8,128)(2,1)} %param.16) | copy-start | bytes 196612
  8.5 81.2 %copy-start.7 = (bf16[1,16,1024]{2,1,0:T(8,128)(2,1)S(1)}, bf16[1,16,1024]{2,1,0:T(8,128)(2,1)}, u32[]{:S(2)}) copy-start(bf16[1,16,1024]{2,1,0:T(8,128)(2,1)} %param.15) | copy-start | bytes 98308
  91.4 9.9 %copy-start.3 = (bf16[1,1024,512]{2,1,0:T(8,128)(2,1)S(1)}, bf16[1,1024,512]{2,1,0:T(8,128)(2,1)}, u32[]{:S(2)}) copy-start(bf16[1,1024,512]{2,1,0:T(8,128)(2,1)} %param.17) | copy-start | bytes 3145732
  91.4 61.2 %all-to-all-start.1 = ((bf16[64,1,16,1024]{3,2,1,0:T(8,128)(2,1)}), bf16[64,1,16,1024]{3,2,1,0:T(8,128)(2,1)S(1)}, u32[]{:S(2)}, u32[]{:S(2)}) async-start(bf16[64,1,16,1024]{3,2,1,0:T(8,128)(2,1)} %stack.2), calls=%async_computation.1 | async-start | bytes 4194304 | tf_op jit(solution)/shard_map/all_to_all | solution.py:12
  101.2 5.2 %copy-start.8 = (s32[1,128,2]{1,2,0:T(2,128)S(1)}, s32[1,128,2]{1,2,0:T(2,128)}, u32[]{:S(2)}) copy-start(s32[1,128,2]{1,2,0:T(2,128)} %param.14) | copy-start | bytes 3076
  101.2 5.6 %copy-start.10 = (s32[1,1,4]{2,1,0:T(1,128)S(1)}, s32[1,1,4]{2,1,0:T(1,128)}, u32[]{:S(2)}) copy-start(s32[1,1,4]{2,1,0:T(1,128)} %param.12) | copy-start | bytes 52
  101.3 5.8 %copy-start.11 = (s32[1,1,4]{2,1,0:T(1,128)S(1)}, s32[1,1,4]{2,1,0:T(1,128)}, u32[]{:S(2)}) copy-start(s32[1,1,4]{2,1,0:T(1,128)} %param.13) | copy-start | bytes 52
  101.3 6.8 %copy-start.9 = (s32[1,2,32]{2,1,0:T(2,128)S(1)}, s32[1,2,32]{2,1,0:T(2,128)}, u32[]{:S(2)}) copy-start(s32[1,2,32]{2,1,0:T(2,128)} %param.11) | copy-start | bytes 772
  104.1 134.6 %collective-permute-start = (bf16[1024,1024]{1,0:T(8,128)(2,1)}, bf16[1024,1024]{1,0:T(8,128)(2,1)}, u32[]{:S(2)}, u32[]{:S(2)}) collective-permute-start(bf16[1024,1024]{1,0:T(8,128)(2,1)} %pad_maximum_fusion.1), channel_id=1, source_target_pairs={{0,1},{1,0},{2,3},{3,2},{4,5},{5,4},{6,7},{7,6},{8,9},{9,8},{10,11... | collective-permute-start | bytes 6291464 | tf_op jit(solution)/shard_map/ppermute | solution.py:26
  157.1 7.9 %copy-start.2 = (bf16[1,512,1024]{2,1,0:T(8,128)(2,1)S(1)}, bf16[1,512,1024]{2,1,0:T(8,128)(2,1)}, u32[]{:S(2)}) copy-start(bf16[1,512,1024]{2,1,0:T(8,128)(2,1)} %param.19) | copy-start | bytes 3145732
  157.1 84.7 %all-to-all-start.2 = ((bf16[64,8,1024]{2,1,0:T(8,128)(2,1)}), bf16[64,8,1024]{2,1,0:T(8,128)(2,1)}, u32[]{:S(2)}, u32[]{:S(2)}) async-start(bf16[64,8,1024]{2,1,0:T(8,128)(2,1)} %bitcast.21), calls=%async_computation.2 | async-start | bytes 2097152 | tf_op jit(solution)/shard_map/all_to_all | solution.py:181
  165.0 69.6 %collective-permute-start.1 = (bf16[512,1024]{1,0:T(8,128)(2,1)S(1)}, bf16[512,1024]{1,0:T(8,128)(2,1)}, u32[]{:S(2)}, u32[]{:S(2)}) collective-permute-start(bf16[512,1024]{1,0:T(8,128)(2,1)S(1)} %bitcast.110), channel_id=1, source_target_pairs={{0,1},{1,0},{2,3},{3,2},{4,5},{5,4},{6,7},{7,6},{8,9},{9,8},{10,11... | collective-permute-start | bytes 3145736 | tf_op jit(solution)/shard_map/ppermute | solution.py:26
  238.7 3.1 %copy-start.4 = (bf16[1,1024,512]{2,1,0:T(8,128)(2,1)S(1)}, bf16[1,1024,512]{2,1,0:T(8,128)(2,1)}, u32[]{:S(2)}) copy-start(bf16[1,1024,512]{2,1,0:T(8,128)(2,1)} %param.17) | copy-start | bytes 3145732
  241.8 3.3 %copy-start.5 = (bf16[1,1024,512]{2,1,0:T(8,128)(2,1)S(1)}, bf16[1,1024,512]{2,1,0:T(8,128)(2,1)}, u32[]{:S(2)}) copy-start(bf16[1,1024,512]{2,1,0:T(8,128)(2,1)} %param.18) | copy-start | bytes 3145732
  241.8 3.3 %copy-start.6 = (bf16[1024,512]{1,0:T(8,128)(2,1)S(1)}, bf16[1024,512]{1,0:T(8,128)(2,1)}, u32[]{:S(2)}) copy-start(bf16[1024,512]{1,0:T(8,128)(2,1)} %get-tuple-element.11) | copy-start | bytes 3145732
  245.1 3.8 %copy-start.1 = (bf16[1024,1024]{1,0:T(8,128)(2,1)S(1)}, bf16[1024,1024]{1,0:T(8,128)(2,1)}, u32[]{:S(2)}) copy-start(bf16[1024,1024]{1,0:T(8,128)(2,1)} %maximum_select_fusion) | copy-start | bytes 6291460
  251.3 40.9 %all-to-all-start.3 = ((bf16[64,8,1024]{2,1,0:T(8,128)(2,1)}), bf16[64,8,1024]{2,1,0:T(8,128)(2,1)S(1)}, u32[]{:S(2)}, u32[]{:S(2)}) async-start(bf16[64,8,1024]{2,1,0:T(8,128)(2,1)} %fusion.16), calls=%async_computation.3 | async-start | bytes 2097152 | tf_op jit(solution)/shard_map/all_to_all | solution.py:183
  295.5 7.0 %collective-permute-start.2 = (bf16[1,128,1024]{2,1,0:T(8,128)(2,1)S(1)}, bf16[1,128,1024]{2,1,0:T(8,128)(2,1)S(1)}, u32[]{:S(2)}, u32[]{:S(2)}) collective-permute-start(bf16[1,128,1024]{2,1,0:T(8,128)(2,1)S(1)} %fusion.35), channel_id=1, source_target_pairs={{448,0},{0,64},{64,128},{128,192},{192,256},{256,320},{320,384},{3... | collective-permute-start | bytes 786440 | tf_op jit(solution)/shard_map/ppermute | solution.py:32
